TPU v7x, 32 devices: a whole 2x2x4 slice. The times are simulated.
32 devices in a mesh: frame: 4 (over z), space: 8 (over y, x, core).
Axes of the slice: x: 2, y: 2, z: 4, core: 2. Of those that a mesh axis runs over, the one named last changes fastest.
Arguments:
- latents: bfloat16 [2, 4, 512, 3072], P(None, 'frame', 'space'), may hold values from -6 to 6
- target: bfloat16 [2, 4, 512, 3072], P(None, 'frame', 'space'), may hold values from -6 to 6
- timesteps: int32 [2], replicated, may hold values from 0 to 999
- valid: int32 [2, 2], replicated, may hold values from 1 to 16, as said below
- tile_mask: int32 [2, 16, 16], replicated, may hold values from 0 to 1, as said below
- w_mod: bfloat16 [256, 18432], replicated, may hold values from -0.5 to 0.5
- w_sqkv: bfloat16 [3, 3072, 2048], P(None, None, 'space'), may hold values from -0.109375 to 0.109375
- w_sout: bfloat16 [2048, 3072], P('space'), may hold values from -0.125 to 0.125
- w_tqkv: bfloat16 [3, 3072, 2048], P(None, None, 'frame'), may hold values from -0.109375 to 0.109375
- w_tout: bfloat16 [2048, 3072], P('frame'), may hold values from -0.125 to 0.125
Outputs:
- mixed: bfloat16 [2, 4, 512, 3072], P(None, 'frame', 'space')
- loss: float32 [], replicated
Inputs may be any that keep to these rules, and one draw needn't show every extreme that they name: Each video's valid frame count is 1 to 4 and valid tile count 1 to 16; video 0 is whole. `tile_mask`: entries are 0 or 1, with ones on the diagonal of every video's mask.
All inputs are finite; a program needn't handle non-finite values.
Results may differ from a plain program's by a relative error of at most 0.017.
Values may be sent and summed in bfloat16 or wider, within the bound.
A program may use at most 128 MiB of HBM per device.

v0:
```python
import math

import jax
import jax.numpy as jnp
from jax import lax
from jax.sharding import PartitionSpec as P

HEAD_DIM = 128
FREQ = 256
TILE = 32


def layer_norm(values):
    mean = jnp.mean(values, -1, keepdims=True)
    centred = values - mean
    var = jnp.mean(centred * centred, -1, keepdims=True)
    return centred * lax.rsqrt(var + 1e-06)


def time_embed(timesteps):
    half = FREQ // 2
    freqs = jnp.exp(-math.log(10000.0) * jnp.arange(half, dtype=jnp.float32) / half)
    angles = timesteps.astype(jnp.float32)[:, None] * freqs[None, :]
    return jnp.concatenate([jnp.cos(angles), jnp.sin(angles)], -1).astype(jnp.bfloat16)


def modulate(values, shift, scale):
    return (
        layer_norm(values.astype(jnp.float32)) * (1.0 + scale[:, None, None, :])
        + shift[:, None, None, :]
    ).astype(jnp.bfloat16)


def frame_attention(qkv, count, tiles, heads):
    length = qkv.shape[0]
    cols = heads * HEAD_DIM
    scale = 1.0 / math.sqrt(HEAD_DIM)
    query = jnp.transpose(qkv[:, :cols].reshape(length, heads, HEAD_DIM), (1, 0, 2))
    keys = jnp.transpose(qkv[:, cols : 2 * cols].reshape(length, heads, HEAD_DIM), (1, 0, 2))
    values = jnp.transpose(qkv[:, 2 * cols :].reshape(length, heads, HEAD_DIM), (1, 0, 2))
    tile_ids = jnp.arange(length, dtype=jnp.int32) // TILE
    expanded = jnp.repeat(jnp.repeat(tiles, TILE, axis=0), TILE, axis=1)
    allowed = (expanded == 1) & (tile_ids[None, :] < count) | (
        tile_ids[:, None] == tile_ids[None, :]
    )

    def one_head(parts):
        q_head, k_head, v_head = parts
        scores = (
            lax.dot_general(
                q_head, k_head, (((1,), (1,)), ((), ())), preferred_element_type=jnp.float32
            )
            * scale
        )
        scores = jnp.where(allowed, scores, -1e30)
        top = jnp.max(scores, -1, keepdims=True)
        weights = jnp.exp(scores - top)
        probs = (weights / jnp.sum(weights, -1, keepdims=True)).astype(jnp.bfloat16)
        return jnp.dot(probs, v_head, preferred_element_type=jnp.float32).astype(jnp.bfloat16)

    outs = lax.map(one_head, (query, keys, values))
    return jnp.transpose(outs, (1, 0, 2)).reshape(length, cols)


def temporal_attention(qkv, count, heads):
    frames, places = (qkv.shape[0], qkv.shape[1])
    cols = heads * HEAD_DIM
    scale = 1.0 / math.sqrt(HEAD_DIM)
    query = qkv[..., :cols].reshape(frames, places, heads, HEAD_DIM)
    keys = qkv[..., cols : 2 * cols].reshape(frames, places, heads, HEAD_DIM)
    values = qkv[..., 2 * cols :].reshape(frames, places, heads, HEAD_DIM)
    scores = jnp.einsum("fphd,gphd->phfg", query, keys, preferred_element_type=jnp.float32) * scale
    frame_ids = jnp.arange(frames, dtype=jnp.int32)
    allowed = (frame_ids[None, :] < count) | (frame_ids[:, None] == frame_ids[None, :])
    scores = jnp.where(allowed, scores, -1e30)
    top = jnp.max(scores, -1, keepdims=True)
    weights = jnp.exp(scores - top)
    probs = (weights / jnp.sum(weights, -1, keepdims=True)).astype(jnp.bfloat16)
    outs = jnp.einsum("phfg,gphd->fphd", probs, values, preferred_element_type=jnp.float32).astype(
        jnp.bfloat16
    )
    return outs.reshape(frames, places, cols)


def group_project(attended, w_out, groups):
    rows = attended.shape[0]
    width = w_out.shape[1]
    parts = attended.reshape(rows, groups, -1)
    weights = w_out.reshape(groups, -1, width)
    terms = jnp.einsum("rgc,gcd->rgd", parts, weights, preferred_element_type=jnp.float32).astype(
        jnp.bfloat16
    )
    return jnp.sum(terms.astype(jnp.float32), axis=1)


def shards(latents, target, timesteps, valid, tile_mask, w_mod, w_sqkv, w_sout, w_tqkv, w_tout):
    videos, frames_dev, span_dev, width = latents.shape
    space_count = lax.axis_size("space")
    frame_count = lax.axis_size("frame")
    embed = time_embed(timesteps)
    mod = jnp.dot(embed, w_mod, preferred_element_type=jnp.float32)
    shift_one, scale_one, gate_one, shift_two, scale_two, gate_two = jnp.split(mod, 6, axis=1)
    h_one = modulate(latents, shift_one, scale_one)
    spatial_heads = w_sqkv.shape[2] // HEAD_DIM
    w_flat = jnp.concatenate([w_sqkv[0], w_sqkv[1], w_sqkv[2]], axis=1)
    qkv_space = jnp.dot(
        lax.all_gather(h_one, "space", axis=2, tiled=True),
        w_flat,
        preferred_element_type=jnp.float32,
    ).astype(jnp.bfloat16)
    span = qkv_space.shape[2]
    frames_flat = qkv_space.reshape(videos * frames_dev, span, -1)
    tile_counts = jnp.repeat(valid[:, 1], frames_dev)
    tiles = jnp.repeat(tile_mask, frames_dev, axis=0)

    def per_frame(parts):
        frame_qkv, count, tiles_one = parts
        return frame_attention(frame_qkv, count, tiles_one, spatial_heads)

    spatial_att = lax.map(per_frame, (frames_flat, tile_counts, tiles)).reshape(
        videos, frames_dev, span, -1
    )
    spatial_att = jnp.transpose(spatial_att, (2, 0, 1, 3))
    w_sall = lax.all_gather(w_sout, "space", axis=0, tiled=True)
    own_rows = lax.all_to_all(spatial_att, "space", split_axis=0, concat_axis=3, tiled=True)
    spatial = group_project(
        own_rows.reshape(span_dev * videos * frames_dev, -1), w_sall, space_count
    )
    spatial = spatial.reshape(span_dev, videos, frames_dev, width)
    spatial = jnp.transpose(spatial, (1, 2, 0, 3))
    x_one = (latents.astype(jnp.float32) + gate_one[:, None, None, :] * spatial).astype(
        jnp.bfloat16
    )
    h_two = modulate(x_one, shift_two, scale_two)
    temporal_heads = w_tqkv.shape[2] // HEAD_DIM
    w_tflat = jnp.concatenate([w_tqkv[0], w_tqkv[1], w_tqkv[2]], axis=1)
    qkv_frame = jnp.dot(
        lax.all_gather(h_two, "frame", axis=1, tiled=True),
        w_tflat,
        preferred_element_type=jnp.float32,
    ).astype(jnp.bfloat16)

    def per_video(parts):
        video_qkv, count = parts
        return temporal_attention(video_qkv, count, temporal_heads)

    temporal_att = lax.map(per_video, (qkv_frame, valid[:, 0]))
    temporal_att = jnp.transpose(temporal_att, (1, 0, 2, 3))
    w_tall = lax.all_gather(w_tout, "frame", axis=0, tiled=True)
    own_frames = lax.all_to_all(temporal_att, "frame", split_axis=0, concat_axis=3, tiled=True)
    temporal = group_project(
        own_frames.reshape(frames_dev * videos * span_dev, -1), w_tall, frame_count
    )
    temporal = temporal.reshape(frames_dev, videos, span_dev, width)
    temporal = jnp.transpose(temporal, (1, 0, 2, 3))
    mixed = (x_one.astype(jnp.float32) + gate_two[:, None, None, :] * temporal).astype(jnp.bfloat16)
    diff = mixed.astype(jnp.float32) - target.astype(jnp.float32)
    squares = jnp.mean(diff * diff, -1)
    frame_ids = lax.axis_index("frame") * frames_dev + jnp.arange(frames_dev, dtype=jnp.int32)
    tile_ids = (lax.axis_index("space") * span_dev + jnp.arange(span_dev, dtype=jnp.int32)) // TILE
    mask = (frame_ids[None, :, None] < valid[:, 0][:, None, None]) & (
        tile_ids[None, None, :] < valid[:, 1][:, None, None]
    )
    local_total = jnp.sum(jnp.where(mask, squares, 0.0))
    total = lax.psum(local_total, ("frame", "space"))
    count = jnp.sum(valid[:, 0] * valid[:, 1]).astype(jnp.float32) * TILE
    return (mixed, total / count)


def solution(mesh):
    return jax.shard_map(
        shards,
        mesh=mesh,
        in_specs=(
            P(None, "frame", "space", None),
            P(None, "frame", "space", None),
            P(),
            P(),
            P(),
            P(),
            P(None, None, "space"),
            P("space", None),
            P(None, None, "frame"),
            P("frame", None),
        ),
        out_specs=(P(None, "frame", "space", None), P()),
        check_vma=False,
    )
```

profile of v0, /device:TPU:0, one launch (start us, length us, event | category | flops | bytes accessed | tf_op | source)
XLA Modules:
  0.0 502.4 jit_solution(8383597021539726154)
XLA Ops:
  7.2 0.7 convert_element_type.72
  8.0 5.1 %fusion.68 = f32[2,18432]{1,0:T(2,128)S(1)} fusion(bf16[256,18432]{1,0:T(8,128)(2,1)} %param.21, bf16[2,128]{1,0:T(2,128)(2,1)S(1)} %get-tuple-element.260, bf16[2,128]{1,0:T(2,128)(2,1)S(1)} %get-tuple-element.259), kind=kOutput, calls=%fused_computation.113 | convolution fusion | flops 18876416 | bytes 9585664 | tf_op jit(solution)/shard_map/dot_general | solution.py:101
  13.3 0.4 fusion.59
  13.7 1.3 fusion.62
  15.1 0.7 all-gather.7.cloned.1.call-update
  16.0 4.4 slice_bitcast_fusion.5
  20.4 43.0 %all-gather.5.cloned.1.call-done = bf16[2,1,512,3072]{3,2,0,1:T(8,128)(2,1)} async-done(((bf16[2,1,64,3072]{3,2,0,1:T(8,128)(2,1)}), bf16[2,1,512,3072]{3,2,0,1:T(8,128)(2,1)}) %all-gather.5.cloned.1.call-update) | async-done | bytes 6291472 | tf_op jit(solution)/shard_map/all_gather | solution.py:107
  63.4 9.9 %fusion.52 = bf16[2,512,768]{2,1,0:T(8,128)(2,1)} fusion(bf16[3072,256]{1,0:T(8,128)(2,1)} %get-tuple-element.251, bf16[3072,256]{1,0:T(8,128)(2,1)} %get-tuple-element.252, bf16[3072,256]{1,0:T(8,128)(2,1)S(1)} %get-tuple-element.250, bf16[2,1,512,3072]{3,2,0,1:T(8,128)(2,1)} %all-gather.5.cloned.1.call-done), kind=kOutput, calls=%fused_computation.84 | convolution fusion | flops 4846780416 | bytes 12582912 | tf_op jit(solution)/shard_map/dot_general | solution.py:106
  73.3 12.7 %while.43 = (s32[]{:T(128)}, bf16[2,512,256]{2,1,0:T(8,128)(2,1)S(1)}, bf16[2,512,768]{2,1,0:T(8,128)(2,1)}, s32[2,16,16]{2,1,0:T(8,128)S(1)}, s32[2]{0:T(128)S(1)}, /*index=5*/s32[]{:T(128)}, s32[]{:T(128)}, s32[]{:T(128)}) while((s32[]{:T(128)}, bf16[2,512,256]{2,1,0:T(8,128)(2,1)S(1)}, bf16[2,512,768]{2,1,0:T(8,128)(2,1)}, ...), condition=%wide.region_7.8_spmd, body=%wide.region_2.7_spmd.sunk | while | flops 137174784 | bytes 10541854 | solution.py:120
  73.3 1.3 constant_dynamic-slice_fusion.4
  75.2 0.6 dynamic_slice.70
  75.8 0.7 broadcast_compare_fusion.3
  76.5 2.7 while.45
  76.5 0.3 fusion.114
  76.8 0.4 fusion.115
  77.4 0.4 fusion.117
  77.8 0.3 fusion.114
  78.1 0.4 fusion.115
  78.7 0.4 fusion.117
  79.7 1.2 constant_dynamic-slice_fusion.4
  81.5 0.6 dynamic_slice.70
  82.1 0.7 broadcast_compare_fusion.3
  82.8 2.7 while.45
  83.1 0.4 fusion.115
  83.7 0.4 fusion.117
  84.1 0.3 fusion.114
  84.4 0.4 fusion.115
  85.0 0.4 fusion.117
  86.0 0.5 copy.99
  86.5 13.3 %all_to_all.30 = bf16[512,2,1,256]{3,1,2,0:T(2,128)(2,1)S(1)} all-to-all(bf16[512,2,1,256]{3,1,2,0:T(2,128)(2,1)S(1)} %bitcast.158), channel_id=1, replica_groups=mesh['frame'=4,'space'=8] {'space'}, dimensions={0} | all-to-all | bytes 1048576 | tf_op jit(solution)/shard_map/all_to_all | solution.py:125
  100.0 42.0 %all-gather.7.cloned.1.call-done = bf16[2048,3072]{1,0:T(8,128)(2,1)} async-done(((bf16[256,3072]{1,0:T(8,128)(2,1)}), bf16[2048,3072]{1,0:T(8,128)(2,1)}) %all-gather.7.cloned.1.call-update) | async-done | bytes 12582928 | tf_op jit(solution)/shard_map/all_gather | solution.py:124
  142.0 7.7 %convert_reduce_fusion = f32[128,3072]{1,0:T(8,128)} fusion(bf16[128,8,256]{2,0,1:T(8,128)(2,1)S(1)} %reshape_reshape.6, bf16[8,256,3072]{2,1,0:T(8,128)(2,1)} %bitcast.152), kind=kOutput, calls=%fused_computation.53 | convolution fusion | flops 1619656704 | bytes 14680064 | tf_op jit(solution)/shard_map/rgc,gcd->rgd/dot_general | solution.py:90
  149.6 2.2 reshape.315
  151.9 0.7 convert_reduce_fusion.2
  152.6 0.4 fusion.55
  152.9 1.3 fusion.58
  154.3 0.5 all-gather.11.cloned.1.call-update
  154.8 6.7 %slice_bitcast_fusion.2 = (bf16[3072,512]{1,0:T(8,128)(2,1)}, bf16[3072,512]{1,0:T(8,128)(2,1)}, bf16[3072,512]{1,0:T(8,128)(2,1)}) fusion(bf16[3,3072,512]{2,1,0:T(8,128)(2,1)} %param.24), kind=kLoop, calls=%fused_computation.72 | loop fusion | bytes 18874368 | tf_op jit(solution)/shard_map/squeeze | solution.py:136
  161.6 56.3 %all-gather.9.cloned.1.call-done = bf16[2,4,64,3072]{3,2,0,1:T(8,128)(2,1)} async-done(((bf16[2,1,64,3072]{3,2,0,1:T(8,128)(2,1)}), bf16[2,4,64,3072]{3,2,0,1:T(8,128)(2,1)}) %all-gather.9.cloned.1.call-update) | async-done | bytes 3145744 | tf_op jit(solution)/shard_map/all_gather | solution.py:138
  217.9 9.7 %fusion.45 = bf16[2,4,64,1536]{3,2,1,0:T(8,128)(2,1)S(1)} fusion(bf16[3072,512]{1,0:T(8,128)(2,1)} %get-tuple-element.248, bf16[3072,512]{1,0:T(8,128)(2,1)} %get-tuple-element.249, bf16[3072,512]{1,0:T(8,128)(2,1)} %get-tuple-element.247, bf16[2,4,64,3072]{3,2,0,1:T(8,128)(2,1)} %all-gather.9.cloned.1.call-done), kind=kOutput, calls=%fused_computation.73 | convolution fusion | flops 4860936192 | bytes 14155776 | tf_op jit(solution)/shard_map/dot_general | solution.py:137
  227.6 11.8 %while.44 = (s32[]{:T(128)}, bf16[2,4,64,512]{3,2,0,1:T(8,128)(2,1)}, bf16[2,4,64,1536]{3,2,1,0:T(8,128)(2,1)S(1)}, s32[2]{0:T(128)S(1)}, s32[]{:T(128)}) while((s32[]{:T(128)}, bf16[2,4,64,512]{3,2,0,1:T(8,128)(2,1)}, bf16[2,4,64,1536]{3,2,1,0:T(8,128)(2,1)S(1)}, s32[2]{0:T(128)S(1)}, s32[]{:T(128)}) %tuple.106), condition=%wide.region_14.15_spmd, body=%wide.region_11.14_spmd.sunk | while | flops 2252841 | bytes 7479929 | solution.py:147
  227.8 0.8 reshape.325
  228.6 1.4 fusion.109
  230.0 0.3 copy.115
  230.4 0.6 dynamic_slice.72
  230.9 0.7 iota_compare_fusion.3
  231.8 0.3 copy.116
  232.1 0.4 fusion.112
  232.8 0.7 bitcast_dynamic-update-slice_fusion.2
  233.8 0.8 reshape.325
  234.5 1.4 fusion.109
  235.9 0.3 copy.115
  236.3 0.6 dynamic_slice.72
  236.9 0.6 iota_compare_fusion.3
  237.7 0.3 copy.116
  238.0 0.4 fusion.112
  238.7 0.7 bitcast_dynamic-update-slice_fusion.2
  239.4 3.7 all-to-all-start.1
  243.1 0.6 multiply_reduce_fusion.1
  244.5 203.0 %all-gather.11.cloned.1.call-done = bf16[2048,3072]{1,0:T(8,128)(2,1)} async-done(((bf16[512,3072]{1,0:T(8,128)(2,1)}), bf16[2048,3072]{1,0:T(8,128)(2,1)}) %all-gather.11.cloned.1.call-update) | async-done | bytes 12582928 | tf_op jit(solution)/shard_map/all_gather | solution.py:149
  447.5 6.6 %convert_reduce_fusion.1 = f32[128,3072]{1,0:T(8,128)S(1)} fusion(bf16[128,4,512]{2,0,1:T(8,128)(2,1)S(1)} %bitcast.157, bf16[4,512,3072]{2,1,0:T(8,128)(2,1)} %bitcast.153), kind=kOutput, calls=%fused_computation.62 | convolution fusion | flops 1614938112 | bytes 14680064 | tf_op jit(solution)/shard_map/rgc,gcd->rgd/dot_general | solution.py:90
  454.1 1.4 multiply_reduce_fusion
  455.5 0.7 fusion.67
  456.1 38.0 %psum.7 = f32[]{:T(128)} all-reduce(f32[]{:T(128)} %fusion.67), channel_id=1, replica_groups=mesh['frame'=4,'space'=8] {'frame','space'}, use_global_device_ids=true, to_apply=%region_18.19 | all-reduce | flops 1 | bytes 8 | tf_op jit(solution)/shard_map/psum | solution.py:165
  (76 shorter events, 5.5 us)
Async XLA Ops:
  7.2 56.2 %all-gather.5.cloned.1.call-start = ((), (), s32[]{:S(2)}) async-start(), calls=%async_computation.2 | async-start | bytes 7077888 | tf_op jit(solution)/shard_map/all_gather | solution.py:107
  8.0 5.1 %copy-start = (bf16[2,1,64,3072]{3,2,1,0:T(8,128)(2,1)S(1)}, bf16[2,1,64,3072]{3,2,1,0:T(8,128)(2,1)}, u32[]{:S(2)}) copy-start(bf16[2,1,64,3072]{3,2,1,0:T(8,128)(2,1)} %param.16) | copy-start | bytes 2359300
  15.0 0.8 copy-start.3
  15.0 126.9 %all-gather.7.cloned.1.call-start = ((), (), s32[]{:S(2)}) async-start(), calls=%async_computation.3 | async-start | bytes 14155776 | tf_op jit(solution)/shard_map/all_gather | solution.py:124
  15.8 202.1 %all-gather.9.cloned.1.call-start = ((), (), s32[]{:S(2)}) async-start(), calls=%async_computation.4 | async-start | bytes 3932160 | tf_op jit(solution)/shard_map/all_gather | solution.py:138
  63.4 9.9 %copy-start.2 = (s32[2,16,16]{2,1,0:T(8,128)S(1)}, s32[2,16,16]{2,1,0:T(8,128)}, u32[]{:S(2)}) copy-start(s32[2,16,16]{2,1,0:T(8,128)} %param.20) | copy-start | bytes 6148
  154.3 293.2 %all-gather.11.cloned.1.call-start = ((), (), s32[]{:S(2)}) async-start(), calls=%async_computation.5 | async-start | bytes 15728640 | tf_op jit(solution)/shard_map/all_gather | solution.py:149
  239.4 208.0 %all-to-all-start.1 = ((bf16[4,2,64,512]{3,2,1,0:T(8,128)(2,1)}), bf16[4,2,64,512]{3,2,1,0:T(8,128)(2,1)S(1)}, u32[]{:S(2)}, u32[]{:S(2)}) async-start(bf16[4,2,64,512]{3,2,1,0:T(8,128)(2,1)} %bitcast.161), calls=%async_computation.1 | async-start | bytes 1048576 | tf_op jit(solution)/shard_map/all_to_all | solution.py:150
  447.5 6.6 %copy-start.1 = (bf16[2,1,64,3072]{3,2,1,0:T(8,128)(2,1)S(1)}, bf16[2,1,64,3072]{3,2,1,0:T(8,128)(2,1)}, u32[]{:S(2)}) copy-start(bf16[2,1,64,3072]{3,2,1,0:T(8,128)(2,1)} %param.17) | copy-start | bytes 2359300
Sparse Core Ops, SparseCore 0:
  15.1 48.2 all-gather.4
  65.3 76.6 all-gather.6
  154.4 63.4 all-gather.8
  219.3 228.0 all-gather.10
where the time goes:
time: 504 us; the launch traced here: 502 us
  waiting for transfers between devices  346 us (69%)
  blocking collectives  51.3 us (10%)
  matrix products  45.9 us (9%)
  local copies, waits for them, and re-layouts  26.5 us (5%)
  between operations  16.3 us (3%)
  other arithmetic  12.6 us (2%)
    all_gather x1, waiting for transfers between devices, shards(): w_tall = lax.all_gather(w_tout, 'frame', axis=0, tiled=True)  203 us
    all_gather x1, waiting for transfers between devices, shards(): lax.all_gather(h_two, 'frame', axis=1, tiled=True)  56.3 us
    all_gather x1, waiting for transfers between devices, shards(): lax.all_gather(h_one, 'space', axis=2, tiled=True)  43 us
    all_gather x1, waiting for transfers between devices, shards(): w_sall = lax.all_gather(w_sout, 'space', axis=0, tiled=True)  42 us
    psum x1, blocking collectives, shards(): total = lax.psum(local_total, ('frame', 'space'))  38 us
    dot_general x2, matrix products, group_project(): jnp.einsum('rgc,gcd->rgd', parts, weights, preferred_element_type=jnp.flo...  14.3 us
    all_to_all x1, blocking collectives, shards(): lax.all_to_all(spatial_att, 'space', split_axis=0, concat_axis=3, tiled=T...  13.3 us
  transfers between devices with their start and end apart: 5, of which 4 were waited for; matrix products, arithmetic and copies ran while one was open for 11% of the time, Pallas kernels for 0%

commit v1 on v0

v1 whole, which is shorter than its diff:
```python
import functools
import math

import jax
import jax.numpy as jnp
from jax import lax
from jax.experimental import pallas as pl
from jax.experimental.pallas import tpu as pltpu
from jax.sharding import PartitionSpec as P

HEAD_DIM = 128
FREQ = 256
TILE = 32
PAD = 128
MESH = pl.DeviceIdType.MESH


def time_embed(timesteps):
    half = FREQ // 2
    freqs = jnp.exp(-math.log(10000.0) * jnp.arange(half, dtype=jnp.float32) / half)
    angles = timesteps.astype(jnp.float32)[:, None] * freqs[None, :]
    return jnp.concatenate([jnp.cos(angles), jnp.sin(angles)], -1).astype(jnp.bfloat16)


def norm_mod(values, shift, scale):
    mean = jnp.mean(values, -1, keepdims=True)
    centred = values - mean
    var = jnp.mean(centred * centred, -1, keepdims=True)
    return (centred * lax.rsqrt(var + 1e-06) * (1.0 + scale) + shift).astype(jnp.bfloat16)


def attend(query, keys, values, allowed):
    scores = lax.dot_general(
        query, keys, (((1,), (1,)), ((), ())), preferred_element_type=jnp.float32
    ) * (1.0 / math.sqrt(HEAD_DIM))
    scores = jnp.where(allowed, scores, -1e30)
    top = jnp.max(scores, -1, keepdims=True)
    weights = jnp.exp(scores - top)
    probs = (weights * (1.0 / jnp.sum(weights, -1, keepdims=True))).astype(jnp.bfloat16)
    return jnp.dot(probs, values, preferred_element_type=jnp.float32).astype(jnp.bfloat16)


def expand(table, ids):
    rows = jnp.dot(ids, table, preferred_element_type=jnp.float32).astype(jnp.bfloat16)
    return lax.dot_general(rows, ids, (((1,), (1,)), ((), ())), preferred_element_type=jnp.float32)


def kernel(
    n_space, n_frame, offsets, nx, ny,
    lat_ref, mod_ref, tiles_ref, framesok_ref, wq_hbm, wso_hbm, wt_hbm,
    x1_ref, att_ref,
    G, PR, R, H, C, wq, wso, wt, qkv, att, tqkv, A, smask, tmask,
    ag_s, ag_r, fw_s, fw_r, pr_s, pr_r, rs_s, rs_r, z_s, z_r, a_s, a_r, w_sem,
):
    V, L, D = lat_ref.shape
    nch = n_space // 2
    span = n_space * L
    sp = lax.axis_index("space")
    fr = lax.axis_index("frame")
    core = sp % 2
    chip = sp // 2
    cx, cy = chip % nx, chip // nx
    no = len(offsets)

    def plus(k):
        dx, dy = offsets[k]
        return ((cy + dy) % ny) * nx + (cx + dx) % nx

    def minus(k):
        dx, dy = offsets[k]
        return ((cy + ny - dy) % ny) * nx + (cx + nx - dx) % nx

    sib = {"space": chip * 2 + (1 - core)}

    loads = [
        pltpu.make_async_copy(wq_hbm, wq, w_sem.at[0]),
        pltpu.make_async_copy(wso_hbm, wso, w_sem.at[1]),
        pltpu.make_async_copy(wt_hbm, wt, w_sem.at[2]),
    ]
    for ld in loads:
        ld.start()

    bar = pltpu.get_barrier_semaphore()
    for k in range(1, no):
        pl.semaphore_signal(bar, inc=1, device_id={"space": plus(k) * 2 + core}, device_id_type=MESH)
    pl.semaphore_signal(bar, inc=1, device_id=sib, device_id_type=MESH)
    for o in range(1, n_frame):
        pl.semaphore_signal(bar, inc=1, device_id={"frame": (fr + o) % n_frame}, device_id_type=MESH)

    def rcopy(src, dst, s, r, dev):
        return pltpu.make_async_remote_copy(
            src_ref=src, dst_ref=dst, send_sem=s, recv_sem=r, device_id=dev, device_id_type=MESH
        )

    def ag(v, k):
        return rcopy(
            G.at[v, chip, core], G.at[v, chip, core], ag_s.at[v, k], ag_r.at[v, k],
            {"space": plus(k) * 2 + core},
        )

    def ag_in(v, k):
        slot = G.at[v, minus(k), core]
        return rcopy(slot, slot, ag_s.at[v, k], ag_r.at[v, k], {"space": plus(k) * 2 + core})

    def fw(v, k):
        slot = G.at[v, minus(k), core]
        return rcopy(slot, slot, fw_s.at[v, k], fw_r.at[v, k], sib)

    def fw_in(v, k):
        slot = G.at[v, minus(k), 1 - core]
        return rcopy(slot, slot, fw_s.at[v, k], fw_r.at[v, k], sib)

    def pr(v, k):
        return rcopy(G.at[v, plus(k), 1 - core], PR.at[v, k], pr_s.at[v, k], pr_r.at[v, k], sib)

    def rs(v, k):
        return rcopy(
            G.at[v, plus(k), core], R.at[v, k], rs_s.at[v, k], rs_r.at[v, k],
            {"space": plus(k) * 2 + core},
        )

    def zg(v, o):
        return rcopy(
            H.at[v, fr], H.at[v, fr], z_s.at[v, o], z_r.at[v, o], {"frame": (fr + o) % n_frame}
        )

    def zg_in(v, o):
        slot = H.at[v, (fr + n_frame - o) % n_frame]
        return rcopy(slot, slot, z_s.at[v, o], z_r.at[v, o], {"frame": (fr + o) % n_frame})

    tc = tqkv.shape[2]

    def ax(v, o):
        cols = pl.ds(pl.multiple_of(fr * tc, tc), tc)
        dst = (fr + o) % n_frame
        return rcopy(
            A.at[v, dst], C.at[v, :, cols], a_s.at[v, o], a_r.at[v, o], {"frame": dst}
        )

    def ax_in(v, o):
        src = (fr + n_frame - o) % n_frame
        cols = pl.ds(pl.multiple_of(src * tc, tc), tc)
        return rcopy(
            A.at[v, src], C.at[v, :, cols], a_s.at[v, o], a_r.at[v, o], {"frame": src}
        )

    def mod(v, i):
        return mod_ref[v, i : i + 1, :]

    for v in range(V):
        G[v, chip, core] = norm_mod(lat_ref[v].astype(jnp.float32), mod(v, 0), mod(v, 1))
        if v == 0:
            pl.semaphore_wait(bar, (no - 1) + 1 + (n_frame - 1))
        for k in range(no - 1, 0, -1):
            ag(v, k).start()
        fw(v, 0).start()

    row = lax.broadcasted_iota(jnp.int32, (span, PAD), 0) // TILE
    col = lax.broadcasted_iota(jnp.int32, (span, PAD), 1)
    tile_ids = (row == col).astype(jnp.bfloat16)
    tl = n_frame * L
    rowf = lax.broadcasted_iota(jnp.int32, (tl, PAD), 0) // L
    colf = lax.broadcasted_iota(jnp.int32, (tl, PAD), 1)
    frame_ids = (rowf == colf).astype(jnp.bfloat16)
    place_q = lax.broadcasted_iota(jnp.int32, (tl, tl), 0) % L
    place_k = lax.broadcasted_iota(jnp.int32, (tl, tl), 1) % L
    for v in range(V):
        smask[v] = expand(tiles_ref[v], tile_ids).astype(jnp.bfloat16)
        both = jnp.where(place_q == place_k, expand(framesok_ref[v], frame_ids), 0.0)
        tmask[v] = both.astype(jnp.bfloat16)

    def forward(v):
        for k in range(1, no):
            ag_in(v, k).wait_recv()
            fw(v, k).start()

    sc = qkv.shape[2]
    QB = 256

    def spatial(v):
        for k in range(no):
            fw_in(v, k).wait_recv()
        if v == 0:
            loads[0].wait()
        mt = 256 // (2 * L)
        nm = nch // mt

        def qkv_step(i, _):
            j, m = i // nm, i % nm
            x = G[v, pl.ds(m * mt, mt)].reshape(256, D)
            qkv[j, pl.ds(pl.multiple_of(m * 256, 256), 256), :] = jnp.dot(
                x, wq[j], preferred_element_type=jnp.float32
            ).astype(jnp.bfloat16)
            return 0

        lax.fori_loop(0, 3 * nm, qkv_step, 0)

        for h in range(sc // HEAD_DIM):
            hs = slice(h * HEAD_DIM, (h + 1) * HEAD_DIM)

            def att_step(i, _):
                rows = pl.ds(pl.multiple_of(i * QB, QB), QB)
                ok = smask[v, rows, :].astype(jnp.float32) > 0.5
                att[rows, hs] = attend(qkv[0, rows, hs], qkv[1, :, hs], qkv[2, :, hs], ok)
                return 0

            lax.fori_loop(0, span // QB, att_step, 0)

        for k in range(1, no):
            ag(v, k).wait_send()
        for k in range(no):
            fw(v, k).wait_send()
        if v == 0:
            loads[1].wait()

        CB = 512

        def term_step(i, _):
            cols = pl.ds(pl.multiple_of(i * CB, CB), CB)
            t = jnp.dot(att[...], wso[:, cols], preferred_element_type=jnp.float32)
            G[v, :, :, :, cols] = t.astype(jnp.bfloat16).reshape(nch, 2, L, CB)
            return 0

        lax.fori_loop(0, D // CB, term_step, 0)
        for k in range(no - 1, -1, -1):
            pr(v, k).start()

    def reduce_send(v):
        for k in range(no - 1, 0, -1):
            pr(v, k).wait_recv()
            c = plus(k)
            G[v, c, core] = (
                G[v, c, core].astype(jnp.float32) + PR[v, k].astype(jnp.float32)
            ).astype(jnp.bfloat16)
            rs(v, k).start()

    def finish_spatial(v):
        pr(v, 0).wait_recv()
        so = G[v, chip, core].astype(jnp.float32) + PR[v, 0].astype(jnp.float32)
        for k in range(1, no):
            rs(v, k).wait_recv()
            so = so + R[v, k].astype(jnp.float32)
        x1 = (lat_ref[v].astype(jnp.float32) + mod(v, 2) * so).astype(jnp.bfloat16)
        x1_ref[v] = x1
        H[v, fr] = norm_mod(x1.astype(jnp.float32), mod(v, 3), mod(v, 4))
        for o in range(1, n_frame):
            zg(v, o).start()

    def temporal(v):
        for o in range(1, n_frame):
            zg_in(v, o).wait_recv()
        if v == 0:
            loads[2].wait()
        NB = 256
        nn = tc // NB

        def tqkv_step(i, _):
            j, n = i // nn, i % nn
            cols = pl.ds(pl.multiple_of(n * NB, NB), NB)
            tqkv[j, :, cols] = jnp.dot(
                H[v].reshape(tl, D), wt[j, :, cols], preferred_element_type=jnp.float32
            ).astype(jnp.bfloat16)
            return 0

        lax.fori_loop(0, 3 * nn, tqkv_step, 0)
        ok = tmask[v].astype(jnp.float32) > 0.5
        for h in range(tc // HEAD_DIM):
            hs = slice(h * HEAD_DIM, (h + 1) * HEAD_DIM)
            out = attend(tqkv[0, :, hs], tqkv[1, :, hs], tqkv[2, :, hs], ok)
            A[v, :, :, hs] = out.reshape(n_frame, L, HEAD_DIM)
        for o in range(1, n_frame):
            ax(v, o).start()
        C[v, :, pl.ds(pl.multiple_of(fr * tc, tc), tc)] = A[v, fr]

    forward(0)
    spatial(0)
    reduce_send(0)
    forward(1)
    spatial(1)
    reduce_send(1)
    finish_spatial(0)
    finish_spatial(1)
    temporal(0)
    temporal(1)
    for v in range(V):
        for o in range(1, n_frame):
            ax_in(v, o).wait_recv()
        att_ref[v] = C[v]
    for v in range(V):
        for k in range(no):
            pr(v, k).wait_send()
        for k in range(1, no):
            rs(v, k).wait_send()
        for o in range(1, n_frame):
            zg(v, o).wait_send()
            ax(v, o).wait_send()


def run_kernel(latents, mod, tiles, frames_ok, w_sqkv, w_sout, w_tqkv):
    V, L, D = latents.shape
    n_space = lax.axis_size("space")
    n_frame = lax.axis_size("frame")
    nch = n_space // 2
    ny = 2 if nch % 2 == 0 else 1
    nx = nch // ny
    offsets = [(dx, dy) for dy in range(ny) for dx in range(nx)]
    no = len(offsets)
    sc, tc = w_sqkv.shape[2], w_tqkv.shape[2]
    span = n_space * L
    tl = n_frame * L
    bf = jnp.bfloat16
    dma = pltpu.SemaphoreType.DMA
    vm = pl.BlockSpec(memory_space=pltpu.VMEM)
    hbm = pl.BlockSpec(memory_space=pl.ANY)
    return pl.pallas_call(
        functools.partial(kernel, n_space, n_frame, offsets, nx, ny),
        out_shape=(
            jax.ShapeDtypeStruct((V, L, D), bf),
            jax.ShapeDtypeStruct((V, L, n_frame * tc), bf),
        ),
        in_specs=[vm, vm, vm, vm, hbm, hbm, hbm],
        out_specs=(vm, vm),
        scratch_shapes=[
            pltpu.VMEM((V, nch, 2, L, D), bf),
            pltpu.VMEM((V, no, L, D), bf),
            pltpu.VMEM((V, no, L, D), bf),
            pltpu.VMEM((V, n_frame, L, D), bf),
            pltpu.VMEM((V, L, n_frame * tc), bf),
            pltpu.VMEM(w_sqkv.shape, bf),
            pltpu.VMEM(w_sout.shape, bf),
            pltpu.VMEM(w_tqkv.shape, bf),
            pltpu.VMEM((3, span, sc), bf),
            pltpu.VMEM((span, sc), bf),
            pltpu.VMEM((3, tl, tc), bf),
            pltpu.VMEM((V, n_frame, L, tc), bf),
            pltpu.VMEM((V, span, span), bf),
            pltpu.VMEM((V, tl, tl), bf),
            dma((V, no)), dma((V, no)), dma((V, no)), dma((V, no)),
            dma((V, no)), dma((V, no)), dma((V, no)), dma((V, no)),
            dma((V, n_frame)), dma((V, n_frame)), dma((V, n_frame)), dma((V, n_frame)),
            dma((3,)),
        ],
        compiler_params=pltpu.CompilerParams(
            collective_id=0, has_side_effects=True, vmem_limit_bytes=60 * 1024 * 1024
        ),
        cost_estimate=pl.CostEstimate(
            flops=20_000_000_000, bytes_accessed=300_000_000, transcendentals=3_000_000
        ),
        name="block",
    )(latents, mod, tiles, frames_ok, w_sqkv, w_sout, w_tqkv)


def shards(latents, target, timesteps, valid, tile_mask, w_mod, w_sqkv, w_sout, w_tqkv, w_tout):
    videos, frames_dev, span_dev, width = latents.shape
    n_frame = lax.axis_size("frame")
    w_tall = lax.all_gather(w_tout, "frame", axis=0, tiled=True)
    embed = time_embed(timesteps)
    mod = jnp.dot(embed, w_mod, preferred_element_type=jnp.float32).reshape(videos, 6, width)
    nt = tile_mask.shape[1]
    t_ids = jnp.arange(nt, dtype=jnp.int32)
    tiles = ((tile_mask == 1) & (t_ids[None, None, :] < valid[:, 1][:, None, None])) | (
        t_ids[None, :, None] == t_ids[None, None, :]
    )
    tiles = jnp.pad(tiles.astype(jnp.bfloat16), ((0, 0), (0, PAD - nt), (0, PAD - nt)))
    p_ids = jnp.arange(PAD, dtype=jnp.int32)
    frames_ok = (
        (p_ids[None, None, :] < valid[:, 0][:, None, None])
        | (p_ids[None, :, None] == p_ids[None, None, :])
    ).astype(jnp.bfloat16)
    x_one, own = run_kernel(
        latents.reshape(videos, span_dev, width), mod, tiles, frames_ok, w_sqkv, w_sout, w_tqkv
    )
    temporal = jnp.dot(
        own.reshape(videos * span_dev, -1), w_tall, preferred_element_type=jnp.float32
    ).reshape(videos, span_dev, width)
    mixed = (x_one.astype(jnp.float32) + mod[:, 5][:, None, :] * temporal).astype(jnp.bfloat16)
    diff = mixed.astype(jnp.float32) - target.reshape(videos, span_dev, width).astype(jnp.float32)
    squares = jnp.mean(diff * diff, -1)
    frame_id = lax.axis_index("frame")
    tile_ids = (lax.axis_index("space") * span_dev + jnp.arange(span_dev, dtype=jnp.int32)) // TILE
    mask = (frame_id < valid[:, 0][:, None]) & (tile_ids[None, :] < valid[:, 1][:, None])
    total = lax.psum(jnp.sum(jnp.where(mask, squares, 0.0)), ("frame", "space"))
    count = jnp.sum(valid[:, 0] * valid[:, 1]).astype(jnp.float32) * TILE
    return (mixed.reshape(latents.shape), total / count)


def solution(mesh):
    return jax.shard_map(
        shards,
        mesh=mesh,
        in_specs=(
            P(None, "frame", "space", None),
            P(None, "frame", "space", None),
            P(),
            P(),
            P(),
            P(),
            P(None, None, "space"),
            P("space", None),
            P(None, None, "frame"),
            P("frame", None),
        ),
        out_specs=(P(None, "frame", "space", None), P()),
        check_vma=False,
    )
```

time: 504 us -> 365 us (0.72)
  waiting for transfers between devices: 346 us -> 55.1 us
  Pallas kernels: 0 us -> 239 us
  matrix products: 45.9 us -> 13 us
  local copies, waits for them, and re-layouts: 26.5 us -> 0.37 us
  blocking collectives: 51.3 us -> 38 us
  other arithmetic: 12.6 us -> 2.4 us
    pallas_call x0 -> x1, Pallas kernels: none -> 239 us  [run_kernel(): pl.pallas_call(functools.partial(kernel, n_space, n_frame, offsets, nx, n...]
    all_gather x1, waiting for transfers between devices: 203 us -> 54.5 us  [shards(): w_tall = lax.all_gather(w_tout, 'frame', axis=0, tiled=True)]
    all_gather x3 -> x0, waiting for transfers between devices: 141 us -> none  [the longest x1 56.3 us: shards(): lax.all_gather(h_two, 'frame', axis=1, tiled=True)]
    dot_general x17 -> x2, matrix products: 45.9 us -> 13 us  [the longest x1 8 us: shards(): jnp.dot(own.reshape(videos * span_dev, -1), w_tall, preferred_element_typ...]
    all_to_all x1 -> x0, blocking collectives: 13.3 us -> none  [shards(): lax.all_to_all(spatial_att, 'space', split_axis=0, concat_axis=3, tiled=T...]
    squeeze x4 -> x0, local copies, waits for them, and re-layouts: 11.2 us -> none  [the longest x1 6.74 us: shards(): w_tflat = jnp.concatenate([w_tqkv[0], w_tqkv[1], w_tqkv[2]], axis=1)]
    dynamic_slice x12 -> x0, local copies, waits for them, and re-layouts: 5.54 us -> none  [shards(): lax.map(per_frame, (frames_flat, tile_counts, tiles))]
  transfers between devices with their start and end apart: 5 -> 1, of which waited for: 4 -> 1; matrix products, arithmetic and copies ran while one was open for 11% -> 2% of each run, Pallas kernels for 0% -> 66%
where the time goes in v1:
time: 365 us; the launch traced here: 364 us
  Pallas kernels  239 us (65%)
  waiting for transfers between devices  55.1 us (15%)
  blocking collectives  38 us (10%)
  between operations  16.6 us (5%)
  matrix products  13 us (4%)
    pallas_call x1, Pallas kernels, run_kernel(): pl.pallas_call(functools.partial(kernel, n_space, n_frame, offsets, nx, n...  239 us
    all_gather x1, waiting for transfers between devices, shards(): w_tall = lax.all_gather(w_tout, 'frame', axis=0, tiled=True)  54.5 us
    psum x1, blocking collectives, shards(): total = lax.psum(jnp.sum(jnp.where(mask, squares, 0.0)), ('frame', 'space'))  38 us
    dot_general x1, matrix products, shards(): jnp.dot(own.reshape(videos * span_dev, -1), w_tall, preferred_element_typ...  8 us
  transfers between devices with their start and end apart: 1, of which 1 were waited for; matrix products, arithmetic and copies ran while one was open for 2% of the time, Pallas kernels for 66%

profile of v1, /device:TPU:0, one launch (start us, length us, event | category | flops | bytes accessed | tf_op | source)
XLA Modules:
  0.0 364.2 jit_solution(1963250135843364142)
XLA Ops:
  7.2 0.0 copy-start.4
  7.2 0.0 all-gather.2.cloned.1.call-start
  7.2 0.7 all-gather.2.cloned.1.call-update
  7.9 0.0 copy-done.4
  7.9 0.1 fusion.13
  8.1 0.0 copy-start.3
  8.1 0.0 copy-start.2
  8.1 5.0 %fusion.16 = f32[2,18432]{1,0:T(2,128)S(1)} fusion(bf16[256,18432]{1,0:T(8,128)(2,1)} %param.15, bf16[2,128]{1,0:T(2,128)(2,1)S(1)} %get-tuple-element.15, bf16[2,128]{1,0:T(2,128)(2,1)S(1)} %get-tuple-element.14), kind=kOutput, calls=%fused_computation.25 | convolution fusion | flops 18876416 | bytes 9585664 | tf_op jit(solution)/shard_map/dot_general | solution.py:358
  13.1 0.1 reshape.122.mod_ref
  13.2 0.0 copy-start.1
  13.3 0.0 copy-done.3
  13.3 0.2 slice_reduce_fusion.1
  13.5 0.6 multiply_reduce_fusion
  14.8 0.1 compare_reduce_fusion
  15.0 0.1 iota_compare_fusion.3
  15.0 0.1 iota_compare_fusion.2
  15.1 0.0 copy-done.2
  15.1 0.7 or_convert_fusion
  15.8 0.0 copy-done.1
  15.8 0.0 copy-start
  15.8 238.6 %block.1 = (bf16[2,64,3072]{2,1,0:T(8,128)(2,1)}, bf16[2,64,2048]{2,1,0:T(8,128)(2,1)}) custom-call(bf16[2,64,3072]{2,1,0:T(8,128)(2,1)} %bitcast.27, f32[2,6,3072]{2,1,0:T(8,128)} %copy-done.1, bf16[2,128,128]{2,1,0:T(8,128)(2,1)} %get-tuple-element.19.tiles_ref, bf16[2,128,128]{2,1,0:T(8,128)(2,1)} %get-tuple-element.18.framesok_ref, ...), custom_call_target="tpu_custom_call" | custom-call | flops 20000000000 | bytes 300000000 | tf_op jit(solution)/shard_map/block/pallas_call | solution.py:315
  254.4 54.5 %all-gather.2.cloned.1.call-done = bf16[2048,3072]{1,0:T(8,128)(2,1)} async-done(((bf16[512,3072]{1,0:T(8,128)(2,1)}), bf16[2048,3072]{1,0:T(8,128)(2,1)}) %all-gather.2.cloned.1.call-update) | async-done | bytes 12582928 | tf_op jit(solution)/shard_map/all_gather | solution.py:356
  308.9 0.0 copy-done
  308.9 8.0 %fusion.12 = (f32[2,64]{1,0:T(2,128)S(1)}, bf16[2,64,3072]{2,1,0:T(8,128)(2,1)}) fusion(bf16[2,1,64,3072]{3,2,1,0:T(8,128)(2,1)S(1)} %copy-done, bf16[2,64,2048]{2,1,0:T(8,128)(2,1)} %get-tuple-element.5, bf16[2048,3072]{1,0:T(8,128)(2,1)} %all-gather.2.cloned.1.call-done, f32[2,3072]{1,0:T(2,128)S(1)} %bitcast.26, bf16[2,64,3072]{2,1,0:T(8,128)(2,1)} %get-tuple-element.4), kind=kOutput, calls=%fused_computation.7 | convolution fusion | flops 1614151552 | bytes 15491584 | tf_op jit(solution)/shard_map/dot_general | solution.py:373
  316.9 0.7 fusion.15
  317.5 38.0 %psum.7 = f32[]{:T(128)} all-reduce(f32[]{:T(128)} %fusion.15), channel_id=1, replica_groups=mesh['frame'=4,'space'=8] {'frame','space'}, use_global_device_ids=true, to_apply=%region_2.3 | all-reduce | flops 1 | bytes 8 | tf_op jit(solution)/shard_map/psum | solution.py:382
  (8 shorter events, 0.1 us)
Async XLA Ops:
  7.2 0.8 copy-start.4
  7.2 301.7 %all-gather.2.cloned.1.call-start = ((), (), s32[]{:S(2)}) async-start(), calls=%async_computation | async-start | bytes 15728640 | tf_op jit(solution)/shard_map/all_gather | solution.py:356
  8.1 5.3 %copy-start.3 = (s32[2,2]{1,0:T(2,128)S(1)}, s32[2,2]{1,0:T(2,128)}, u32[]{:S(2)}) copy-start(s32[2,2]{1,0:T(2,128)} %param.13) | copy-start | bytes 52
  8.1 7.1 %copy-start.2 = (s32[2,16,16]{2,1,0:T(8,128)S(1)}, s32[2,16,16]{2,1,0:T(8,128)}, u32[]{:S(2)}) copy-start(s32[2,16,16]{2,1,0:T(8,128)} %param.14) | copy-start | bytes 6148
  13.2 2.6 copy-start.1
  15.8 293.1 %copy-start = (bf16[2,1,64,3072]{3,2,1,0:T(8,128)(2,1)S(1)}, bf16[2,1,64,3072]{3,2,1,0:T(8,128)(2,1)}, u32[]{:S(2)}) copy-start(bf16[2,1,64,3072]{3,2,1,0:T(8,128)(2,1)} %param.11) | copy-start | bytes 2359300
Sparse Core Ops, SparseCore 0:
  9.6 299.2 all-gather.1

commit v2 on v1

--- a/solution.py
+++ b/solution.py
@@ -47,10 +47,11 @@
 
 def kernel(
     n_space, n_frame, offsets, nx, ny,
-    lat_ref, mod_ref, tiles_ref, framesok_ref, wq_hbm, wso_hbm, wt_hbm,
-    x1_ref, att_ref,
-    G, PR, R, H, C, wq, wso, wt, qkv, att, tqkv, A, smask, tmask,
-    ag_s, ag_r, fw_s, fw_r, pr_s, pr_r, rs_s, rs_r, z_s, z_r, a_s, a_r, w_sem,
+    lat_ref, mod_ref, tiles_ref, framesok_ref, tokw_ref, wq_hbm, wso_hbm, wt_hbm, wto_hbm, tgt_hbm,
+    mixed_ref, loss_ref, W,
+    G, PR, R, H, C, x1_ref, tgt, LS, LF, wq, wso, wt, qkv, att, tqkv, A, smask, tmask,
+    ag_s, ag_r, fw_s, fw_r, pr_s, pr_r, rs_s, rs_r, z_s, z_r, a_s, a_r,
+    wz_s, wz_r, wp_s, wp_r, ws_s, ws_r, l_s, l_r, lf_s, lf_r, w_sem, wl_sem,
 ):
     V, L, D = lat_ref.shape
     nch = n_space // 2
@@ -70,20 +71,30 @@
         dx, dy = offsets[k]
         return ((cy + ny - dy) % ny) * nx + (cx + nx - dx) % nx
 
+    FR = wto_hbm.shape[0]
+    U = FR // n_space
+
+    def frame_rows(f):
+        return pl.ds(pl.multiple_of(f * FR, FR), FR)
+
+    def unit(f, s):
+        return W.at[pl.ds(pl.multiple_of(f * FR + s * U, U), U)]
+
     sib = {"space": chip * 2 + (1 - core)}
 
     loads = [
         pltpu.make_async_copy(wq_hbm, wq, w_sem.at[0]),
         pltpu.make_async_copy(wso_hbm, wso, w_sem.at[1]),
         pltpu.make_async_copy(wt_hbm, wt, w_sem.at[2]),
+        pltpu.make_async_copy(tgt_hbm, tgt, w_sem.at[3]),
+        pltpu.make_async_copy(wto_hbm, W.at[frame_rows(fr)], w_sem.at[4]),
     ]
     for ld in loads:
         ld.start()
 
     bar = pltpu.get_barrier_semaphore()
-    for k in range(1, no):
-        pl.semaphore_signal(bar, inc=1, device_id={"space": plus(k) * 2 + core}, device_id_type=MESH)
-    pl.semaphore_signal(bar, inc=1, device_id=sib, device_id_type=MESH)
+    for o in range(1, n_space):
+        pl.semaphore_signal(bar, inc=1, device_id={"space": (sp + o) % n_space}, device_id_type=MESH)
     for o in range(1, n_frame):
         pl.semaphore_signal(bar, inc=1, device_id={"frame": (fr + o) % n_frame}, device_id_type=MESH)
 
@@ -144,16 +155,62 @@
             A.at[v, src], C.at[v, :, cols], a_s.at[v, o], a_r.at[v, o], {"frame": src}
         )
 
+    def wz(o):
+        src = wto_hbm.at[pl.ds(pl.multiple_of(sp * U, U), U)]
+        return rcopy(
+            src, unit(fr, sp), wz_s.at[o], wz_r.at[o], {"frame": (fr + o) % n_frame}
+        )
+
+    def wz_in(o):
+        slot = unit((fr + n_frame - o) % n_frame, sp)
+        return rcopy(slot, slot, wz_s.at[o], wz_r.at[o], {"frame": (fr + o) % n_frame})
+
+    def wp(o, k):
+        slot = unit((fr + n_frame - o) % n_frame, sp)
+        return rcopy(slot, slot, wp_s.at[o, k], wp_r.at[o, k], {"space": plus(k) * 2 + core})
+
+    def wp_in(o, k):
+        slot = unit((fr + n_frame - o) % n_frame, minus(k) * 2 + core)
+        return rcopy(slot, slot, wp_s.at[o, k], wp_r.at[o, k], {"space": plus(k) * 2 + core})
+
+    def ws(o, k):
+        slot = unit((fr + n_frame - o) % n_frame, minus(k) * 2 + core)
+        return rcopy(slot, slot, ws_s.at[o, k], ws_r.at[o, k], sib)
+
+    def ws_in(o, k):
+        slot = unit((fr + n_frame - o) % n_frame, minus(k) * 2 + 1 - core)
+        return rcopy(slot, slot, ws_s.at[o, k], ws_r.at[o, k], sib)
+
+    def ls(o):
+        return rcopy(
+            LS.at[sp], LS.at[sp], l_s.at[o], l_r.at[o], {"space": (sp + o) % n_space}
+        )
+
+    def ls_in(o):
+        slot = LS.at[(sp + n_space - o) % n_space]
+        return rcopy(slot, slot, l_s.at[o], l_r.at[o], {"space": (sp + o) % n_space})
+
+    def lf(o):
+        return rcopy(
+            LF.at[fr], LF.at[fr], lf_s.at[o], lf_r.at[o], {"frame": (fr + o) % n_frame}
+        )
+
+    def lf_in(o):
+        slot = LF.at[(fr + n_frame - o) % n_frame]
+        return rcopy(slot, slot, lf_s.at[o], lf_r.at[o], {"frame": (fr + o) % n_frame})
+
     def mod(v, i):
         return mod_ref[v, i : i + 1, :]
 
     for v in range(V):
         G[v, chip, core] = norm_mod(lat_ref[v].astype(jnp.float32), mod(v, 0), mod(v, 1))
         if v == 0:
-            pl.semaphore_wait(bar, (no - 1) + 1 + (n_frame - 1))
+            pl.semaphore_wait(bar, (n_space - 1) + (n_frame - 1))
         for k in range(no - 1, 0, -1):
             ag(v, k).start()
         fw(v, 0).start()
+    for o in range(1, n_frame):
+        wz(o).start()
 
     row = lax.broadcasted_iota(jnp.int32, (span, PAD), 0) // TILE
     col = lax.broadcasted_iota(jnp.int32, (span, PAD), 1)
@@ -280,23 +337,99 @@
     reduce_send(1)
     finish_spatial(0)
     finish_spatial(1)
+    for o in range(1, n_frame):
+        wz_in(o).wait_recv()
+        for k in range(no - 1, 0, -1):
+            wp(o, k).start()
+        ws(o, 0).start()
     temporal(0)
+    for o in range(1, n_frame):
+        for k in range(1, no):
+            wp_in(o, k).wait_recv()
+            ws(o, k).start()
     temporal(1)
-    for v in range(V):
-        for o in range(1, n_frame):
-            ax_in(v, o).wait_recv()
-        att_ref[v] = C[v]
+
     for v in range(V):
         for k in range(no):
             pr(v, k).wait_send()
         for k in range(1, no):
             rs(v, k).wait_send()
+    for o in range(1, n_frame):
+        for k in range(no):
+            ws_in(o, k).wait_recv()
+    loads[4].wait()
+    rows = FR * n_frame
+    slots = [G.at[v, c, e] for v in range(V) for c in range(nch) for e in range(2)]
+    slots += [PR.at[v, k] for v in range(V) for k in range(no)]
+    slots += [R.at[v, k] for v in range(V) for k in range(no)]
+    pulls = [
+        pltpu.make_async_copy(W.at[pl.ds(b * L, L)], slots[b], wl_sem.at[b])
+        for b in range(rows // L)
+    ]
+    for p in pulls:
+        p.start()
+    quads = [(G, v, c) for v in range(V) for c in range(0, nch, 2)]
+    quads += [(PR, v, k) for v in range(V) for k in range(0, no, 4)]
+    quads += [(R, v, k) for v in range(V) for k in range(0, no, 4)]
+    quads = quads[: rows // (4 * L)]
+    for v in range(V):
+        for o in range(1, n_frame):
+            ax_in(v, o).wait_recv()
+    loads[3].wait()
+    for p in pulls:
+        p.wait()
+    CB = 512
+
+    def out_step(i, total):
+        cols = pl.ds(pl.multiple_of(i * CB, CB), CB)
+        acc = jnp.zeros((V * L, CB), jnp.float32)
+        for q, (buf, v, c) in enumerate(quads):
+            if buf is G:
+                w = buf[v, c : c + 2, :, :, cols].reshape(4 * L, CB)
+            else:
+                w = buf[v, c : c + 4, :, cols].reshape(4 * L, CB)
+            a = C[:, :, q * 4 * L : (q + 1) * 4 * L].reshape(V * L, 4 * L)
+            acc = acc + jnp.dot(a, w, preferred_element_type=jnp.float32)
+        part = []
+        for v in range(V):
+            gate = mod_ref[v, 5:6, cols]
+            m = x1_ref[v, :, cols].astype(jnp.float32) + gate * acc[v * L : (v + 1) * L]
+            m = m.astype(jnp.bfloat16)
+            mixed_ref[v, :, cols] = m
+            diff = m.astype(jnp.float32) - tgt[v, :, cols].astype(jnp.float32)
+            part.append(jnp.sum(diff * diff, -1, keepdims=True))
+        return total + jnp.concatenate(part, 0)
+
+    squares = lax.fori_loop(0, D // CB, out_step, jnp.zeros((V * L, 1), jnp.float32)) * (1.0 / D)
+    kept = squares.reshape(V, L, 1) * tokw_ref[...]
+    LS[sp] = jnp.broadcast_to(jnp.sum(jnp.sum(kept, 0), 0, keepdims=True), (8, 128))
+    for o in range(1, n_space):
+        ls(o).start()
+    for o in range(1, n_space):
+        ls_in(o).wait_recv()
+    LF[fr] = jnp.sum(LS[...], 0)
+    for o in range(1, n_frame):
+        lf(o).start()
+    for o in range(1, n_frame):
+        lf_in(o).wait_recv()
+    loss_ref[...] = jnp.sum(LF[...], 0)
+
+    for v in range(V):
         for o in range(1, n_frame):
             zg(v, o).wait_send()
             ax(v, o).wait_send()
-
-
-def run_kernel(latents, mod, tiles, frames_ok, w_sqkv, w_sout, w_tqkv):
+    for o in range(1, n_frame):
+        wz(o).wait_send()
+        lf(o).wait_send()
+        for k in range(no):
+            ws(o, k).wait_send()
+        for k in range(1, no):
+            wp(o, k).wait_send()
+    for o in range(1, n_space):
+        ls(o).wait_send()
+
+
+def run_kernel(latents, mod, tiles, frames_ok, tokw, w_sqkv, w_sout, w_tqkv, w_tout, target):
     V, L, D = latents.shape
     n_space = lax.axis_size("space")
     n_frame = lax.axis_size("frame")
@@ -316,16 +449,21 @@
         functools.partial(kernel, n_space, n_frame, offsets, nx, ny),
         out_shape=(
             jax.ShapeDtypeStruct((V, L, D), bf),
-            jax.ShapeDtypeStruct((V, L, n_frame * tc), bf),
+            jax.ShapeDtypeStruct((8, 128), jnp.float32),
+            jax.ShapeDtypeStruct((n_frame * w_tout.shape[0], D), bf),
         ),
-        in_specs=[vm, vm, vm, vm, hbm, hbm, hbm],
-        out_specs=(vm, vm),
+        in_specs=[vm, vm, vm, vm, vm, hbm, hbm, hbm, hbm, hbm],
+        out_specs=(vm, vm, hbm),
         scratch_shapes=[
             pltpu.VMEM((V, nch, 2, L, D), bf),
             pltpu.VMEM((V, no, L, D), bf),
             pltpu.VMEM((V, no, L, D), bf),
             pltpu.VMEM((V, n_frame, L, D), bf),
             pltpu.VMEM((V, L, n_frame * tc), bf),
+            pltpu.VMEM((V, L, D), bf),
+            pltpu.VMEM((V, L, D), bf),
+            pltpu.VMEM((n_space, 8, 128), jnp.float32),
+            pltpu.VMEM((n_frame, 8, 128), jnp.float32),
             pltpu.VMEM(w_sqkv.shape, bf),
             pltpu.VMEM(w_sout.shape, bf),
             pltpu.VMEM(w_tqkv.shape, bf),
@@ -338,7 +476,9 @@
             dma((V, no)), dma((V, no)), dma((V, no)), dma((V, no)),
             dma((V, no)), dma((V, no)), dma((V, no)), dma((V, no)),
             dma((V, n_frame)), dma((V, n_frame)), dma((V, n_frame)), dma((V, n_frame)),
-            dma((3,)),
+            dma((n_frame,)), dma((n_frame,)), dma((n_frame, no)), dma((n_frame, no)),
+            dma((n_frame, no)), dma((n_frame, no)), dma((n_space,)), dma((n_space,)),
+            dma((n_frame,)), dma((n_frame,)), dma((5,)), dma((n_frame * w_tout.shape[0] // L,)),
         ],
         compiler_params=pltpu.CompilerParams(
             collective_id=0, has_side_effects=True, vmem_limit_bytes=60 * 1024 * 1024
@@ -347,13 +487,11 @@
             flops=20_000_000_000, bytes_accessed=300_000_000, transcendentals=3_000_000
         ),
         name="block",
-    )(latents, mod, tiles, frames_ok, w_sqkv, w_sout, w_tqkv)
+    )(latents, mod, tiles, frames_ok, tokw, w_sqkv, w_sout, w_tqkv, w_tout, target)
 
 
 def shards(latents, target, timesteps, valid, tile_mask, w_mod, w_sqkv, w_sout, w_tqkv, w_tout):
     videos, frames_dev, span_dev, width = latents.shape
-    n_frame = lax.axis_size("frame")
-    w_tall = lax.all_gather(w_tout, "frame", axis=0, tiled=True)
     embed = time_embed(timesteps)
     mod = jnp.dot(embed, w_mod, preferred_element_type=jnp.float32).reshape(videos, 6, width)
     nt = tile_mask.shape[1]
@@ -367,21 +505,18 @@
         (p_ids[None, None, :] < valid[:, 0][:, None, None])
         | (p_ids[None, :, None] == p_ids[None, None, :])
     ).astype(jnp.bfloat16)
-    x_one, own = run_kernel(
-        latents.reshape(videos, span_dev, width), mod, tiles, frames_ok, w_sqkv, w_sout, w_tqkv
+    tile_ids = (lax.axis_index("space") * span_dev + jnp.arange(span_dev, dtype=jnp.int32)) // TILE
+    mask = (lax.axis_index("frame") < valid[:, 0][:, None]) & (
+        tile_ids[None, :] < valid[:, 1][:, None]
     )
-    temporal = jnp.dot(
-        own.reshape(videos * span_dev, -1), w_tall, preferred_element_type=jnp.float32
-    ).reshape(videos, span_dev, width)
-    mixed = (x_one.astype(jnp.float32) + mod[:, 5][:, None, :] * temporal).astype(jnp.bfloat16)
-    diff = mixed.astype(jnp.float32) - target.reshape(videos, span_dev, width).astype(jnp.float32)
-    squares = jnp.mean(diff * diff, -1)
-    frame_id = lax.axis_index("frame")
-    tile_ids = (lax.axis_index("space") * span_dev + jnp.arange(span_dev, dtype=jnp.int32)) // TILE
-    mask = (frame_id < valid[:, 0][:, None]) & (tile_ids[None, :] < valid[:, 1][:, None])
-    total = lax.psum(jnp.sum(jnp.where(mask, squares, 0.0)), ("frame", "space"))
+    tokw = jnp.broadcast_to(mask.astype(jnp.float32)[:, :, None], (videos, span_dev, 128))
+    shape = (videos, span_dev, width)
+    mixed, total, _ = run_kernel(
+        latents.reshape(shape), mod, tiles, frames_ok, tokw,
+        w_sqkv, w_sout, w_tqkv, w_tout, target.reshape(shape),
+    )
     count = jnp.sum(valid[:, 0] * valid[:, 1]).astype(jnp.float32) * TILE
-    return (mixed.reshape(latents.shape), total / count)
+    return (mixed.reshape(latents.shape), total[0, 0] / count)
 
 
 def solution(mesh):

time: 365 us -> 174 us (0.48)
  Pallas kernels: 239 us -> 156 us
  waiting for transfers between devices: 55.1 us -> 0 us
  blocking collectives: 38 us -> 0 us
  between operations: 16.6 us -> 3.1 us
  matrix products: 13 us -> 5.01 us
  local copies, waits for them, and re-layouts: 0.37 us -> 5.74 us
    pallas_call x1, Pallas kernels: 239 us -> 156 us  [run_kernel(): pl.pallas_call(functools.partial(kernel, n_space, n_frame, offsets, nx, n...]
    all_gather x1 -> x0, waiting for transfers between devices: 54.5 us -> none  [shards(): w_tall = lax.all_gather(w_tout, 'frame', axis=0, tiled=True)]
    psum x1 -> x0, blocking collectives: 38 us -> none  [shards(): total = lax.psum(jnp.sum(jnp.where(mask, squares, 0.0)), ('frame', 'space'))]
    dot_general x1 -> x0, matrix products: 8 us -> none  [shards(): jnp.dot(own.reshape(videos * span_dev, -1), w_tall, preferred_element_typ...]
  transfers between devices with their start and end apart: 1 -> 0, of which waited for: 1 -> 0; matrix products, arithmetic and copies ran while one was open for 2% -> 0% of each run, Pallas kernels for 66% -> 0%
where the time goes in v2:
time: 174 us
  Pallas kernels  156 us (90%)
  local copies, waits for them, and re-layouts  5.74 us (3%)
  matrix products  5.01 us (3%)
  other arithmetic  3.86 us (2%)
  between operations  3.1 us (2%)
    pallas_call x1, Pallas kernels, run_kernel(): pl.pallas_call(functools.partial(kernel, n_space, n_frame, offsets, nx, n...  156 us
    dot_general x1, matrix products, shards(): jnp.dot(embed, w_mod, preferred_element_type=jnp.float32)  5.01 us

profile of v2, /device:TPU:0, one launch (start us, length us, event | category | flops | bytes accessed | tf_op | source)
XLA Modules:
  0.0 173.7 jit_solution(13928497766211379872)
XLA Ops:
  0.6 0.8 compare_reduce_fusion
  1.4 0.7 convert_element_type.20
  2.1 0.1 fusion
  2.2 1.0 slice_reduce_fusion.1
  3.2 0.6 multiply_reduce_fusion
  4.5 0.1 iota_compare_fusion.2
  4.6 0.1 and_convert_fusion
  4.6 0.1 iota_compare_fusion.3
  4.7 0.7 and_or_fusion
  5.5 0.7 broadcast_in_dim.2.tokw_ref
  6.2 0.7 or_convert_fusion
  6.8 5.0 %fusion.2 = f32[2,18432]{1,0:T(2,128)S(1)} fusion(bf16[256,18432]{1,0:T(8,128)(2,1)} %param.15, bf16[2,128]{1,0:T(2,128)(2,1)S(1)} %get-tuple-element.13, bf16[2,128]{1,0:T(2,128)(2,1)S(1)} %get-tuple-element.12), kind=kOutput, calls=%fused_computation.15 | convolution fusion | flops 18876416 | bytes 9585664 | tf_op jit(solution)/shard_map/dot_general | solution.py:496
  11.8 0.8 reshape.165.mod_ref
  12.7 156.0 %block.1 = (bf16[2,64,3072]{2,1,0:T(8,128)(2,1)}, f32[8,128]{1,0:T(8,128)}, bf16[2048,3072]{1,0:T(8,128)(2,1)}) custom-call(bf16[2,64,3072]{2,1,0:T(8,128)(2,1)} %bitcast.8, f32[2,6,3072]{2,1,0:T(8,128)} %reshape.165.mod_ref, bf16[2,128,128]{2,1,0:T(8,128)(2,1)} %get-tuple-element.15.tiles_ref, bf16[2,128,128]{2,1,0:T(8,128)(2,1)} %get-tuple-element.14.framesok_ref, ...), custom_call_target="tpu_custom_call" | custom-call | flops 20000000000 | bytes 300000000 | tf_op jit(solution)/shard_map/block/pallas_call | solution.py:448
  168.7 1.2 slice.15
  170.5 2.1 %copy.15 = bf16[2,1,64,3072]{3,2,1,0:T(8,128)(2,1)} copy(bf16[2,1,64,3072]{3,2,1,0:T(8,128)(2,1)} %bitcast.7) | data formatting | bytes 1572864
  (4 shorter events, 0.0 us)

commit v3 on v2

--- a/solution.py
+++ b/solution.py
@@ -74,9 +74,6 @@
     FR = wto_hbm.shape[0]
     U = FR // n_space
 
-    def frame_rows(f):
-        return pl.ds(pl.multiple_of(f * FR, FR), FR)
-
     def unit(f, s):
         return W.at[pl.ds(pl.multiple_of(f * FR + s * U, U), U)]
 
@@ -87,7 +84,6 @@
         pltpu.make_async_copy(wso_hbm, wso, w_sem.at[1]),
         pltpu.make_async_copy(wt_hbm, wt, w_sem.at[2]),
         pltpu.make_async_copy(tgt_hbm, tgt, w_sem.at[3]),
-        pltpu.make_async_copy(wto_hbm, W.at[frame_rows(fr)], w_sem.at[4]),
     ]
     for ld in loads:
         ld.start()
@@ -357,13 +353,21 @@
     for o in range(1, n_frame):
         for k in range(no):
             ws_in(o, k).wait_recv()
-    loads[4].wait()
     rows = FR * n_frame
     slots = [G.at[v, c, e] for v in range(V) for c in range(nch) for e in range(2)]
     slots += [PR.at[v, k] for v in range(V) for k in range(no)]
     slots += [R.at[v, k] for v in range(V) for k in range(no)]
+
+    def from_frame(row):
+        start = ((fr + n_frame - row // FR) % n_frame) * FR + row % FR
+        return pl.multiple_of(start, L)
+
     pulls = [
-        pltpu.make_async_copy(W.at[pl.ds(b * L, L)], slots[b], wl_sem.at[b])
+        pltpu.make_async_copy(
+            wto_hbm.at[pl.ds(b * L, L)] if b * L < FR else W.at[pl.ds(from_frame(b * L), L)],
+            slots[b],
+            wl_sem.at[b],
+        )
         for b in range(rows // L)
     ]
     for p in pulls:
@@ -388,7 +392,8 @@
                 w = buf[v, c : c + 2, :, :, cols].reshape(4 * L, CB)
             else:
                 w = buf[v, c : c + 4, :, cols].reshape(4 * L, CB)
-            a = C[:, :, q * 4 * L : (q + 1) * 4 * L].reshape(V * L, 4 * L)
+            mine = pl.ds(pl.multiple_of(from_frame(q * 4 * L), 4 * L), 4 * L)
+            a = C[:, :, mine].reshape(V * L, 4 * L)
             acc = acc + jnp.dot(a, w, preferred_element_type=jnp.float32)
         part = []
         for v in range(V):
@@ -478,7 +483,7 @@
             dma((V, n_frame)), dma((V, n_frame)), dma((V, n_frame)), dma((V, n_frame)),
             dma((n_frame,)), dma((n_frame,)), dma((n_frame, no)), dma((n_frame, no)),
             dma((n_frame, no)), dma((n_frame, no)), dma((n_space,)), dma((n_space,)),
-            dma((n_frame,)), dma((n_frame,)), dma((5,)), dma((n_frame * w_tout.shape[0] // L,)),
+            dma((n_frame,)), dma((n_frame,)), dma((4,)), dma((n_frame * w_tout.shape[0] // L,)),
         ],
         compiler_params=pltpu.CompilerParams(
             collective_id=0, has_side_effects=True, vmem_limit_bytes=60 * 1024 * 1024

time: 174 us -> 174 us (level)
  no operation moved by 1% of the time
where the time goes in v3:
time: 174 us
  Pallas kernels  156 us (90%)
  local copies, waits for them, and re-layouts  5.74 us (3%)
  matrix products  5.01 us (3%)
  other arithmetic  3.86 us (2%)
  between operations  3.1 us (2%)
    pallas_call x1, Pallas kernels, run_kernel(): pl.pallas_call(functools.partial(kernel, n_space, n_frame, offsets, nx, n...  156 us
    dot_general x1, matrix products, shards(): jnp.dot(embed, w_mod, preferred_element_type=jnp.float32)  5.01 us

profile of v3, /device:TPU:0, one launch (start us, length us, event | category | flops | bytes accessed | tf_op | source)
XLA Modules:
  0.0 173.7 jit_solution(1734819580115644678)
XLA Ops:
  0.6 0.8 compare_reduce_fusion
  1.4 0.7 convert_element_type.20
  2.1 0.1 fusion
  2.2 1.0 slice_reduce_fusion.1
  3.2 0.6 multiply_reduce_fusion
  4.5 0.1 iota_compare_fusion.2
  4.6 0.1 and_convert_fusion
  4.6 0.1 iota_compare_fusion.3
  4.7 0.7 and_or_fusion
  5.5 0.7 broadcast_in_dim.2.tokw_ref
  6.2 0.7 or_convert_fusion
  6.8 5.0 %fusion.2 = f32[2,18432]{1,0:T(2,128)S(1)} fusion(bf16[256,18432]{1,0:T(8,128)(2,1)} %param.15, bf16[2,128]{1,0:T(2,128)(2,1)S(1)} %get-tuple-element.13, bf16[2,128]{1,0:T(2,128)(2,1)S(1)} %get-tuple-element.12), kind=kOutput, calls=%fused_computation.15 | convolution fusion | flops 18876416 | bytes 9585664 | tf_op jit(solution)/shard_map/dot_general | solution.py:501
  11.8 0.8 reshape.165.mod_ref
  12.7 156.0 %block.1 = (bf16[2,64,3072]{2,1,0:T(8,128)(2,1)}, f32[8,128]{1,0:T(8,128)}, bf16[2048,3072]{1,0:T(8,128)(2,1)}) custom-call(bf16[2,64,3072]{2,1,0:T(8,128)(2,1)} %bitcast.8, f32[2,6,3072]{2,1,0:T(8,128)} %reshape.165.mod_ref, bf16[2,128,128]{2,1,0:T(8,128)(2,1)} %get-tuple-element.15.tiles_ref, bf16[2,128,128]{2,1,0:T(8,128)(2,1)} %get-tuple-element.14.framesok_ref, ...), custom_call_target="tpu_custom_call" | custom-call | flops 20000000000 | bytes 300000000 | tf_op jit(solution)/shard_map/block/pallas_call | solution.py:453
  168.6 1.2 slice.15
  170.5 2.1 %copy.15 = bf16[2,1,64,3072]{3,2,1,0:T(8,128)(2,1)} copy(bf16[2,1,64,3072]{3,2,1,0:T(8,128)(2,1)} %bitcast.7) | data formatting | bytes 1572864
  (4 shorter events, 0.0 us)

commit v4 on v3

--- a/solution.py
+++ b/solution.py
@@ -329,9 +329,9 @@
     spatial(0)
     reduce_send(0)
     forward(1)
+    finish_spatial(0)
     spatial(1)
     reduce_send(1)
-    finish_spatial(0)
     finish_spatial(1)
     for o in range(1, n_frame):
         wz_in(o).wait_recv()

time: 174 us -> 184 us (1.057)
  Pallas kernels: 156 us -> 166 us
    pallas_call x1, Pallas kernels: 156 us -> 166 us  [run_kernel(): pl.pallas_call(functools.partial(kernel, n_space, n_frame, offsets, nx, n...]
where the time goes in v4:
time: 184 us
  Pallas kernels  166 us (90%)
  local copies, waits for them, and re-layouts  5.74 us (3%)
  matrix products  5.01 us (3%)
  other arithmetic  3.86 us (2%)
  between operations  3.1 us (2%)
    pallas_call x1, Pallas kernels, run_kernel(): pl.pallas_call(functools.partial(kernel, n_space, n_frame, offsets, nx, n...  166 us
    dot_general x1, matrix products, shards(): jnp.dot(embed, w_mod, preferred_element_type=jnp.float32)  5.01 us

profile of v4, /device:TPU:0, one launch (start us, length us, event | category | flops | bytes accessed | tf_op | source)
XLA Modules:
  0.0 184.0 jit_solution(1859088445055259433)
XLA Ops:
  0.6 0.8 compare_reduce_fusion
  1.4 0.7 convert_element_type.20
  2.1 0.1 fusion
  2.2 1.0 slice_reduce_fusion.1
  3.2 0.6 multiply_reduce_fusion
  4.5 0.1 iota_compare_fusion.2
  4.6 0.1 and_convert_fusion
  4.6 0.1 iota_compare_fusion.3
  4.7 0.7 and_or_fusion
  5.5 0.7 broadcast_in_dim.2.tokw_ref
  6.2 0.7 or_convert_fusion
  6.8 5.0 %fusion.2 = f32[2,18432]{1,0:T(2,128)S(1)} fusion(bf16[256,18432]{1,0:T(8,128)(2,1)} %param.15, bf16[2,128]{1,0:T(2,128)(2,1)S(1)} %get-tuple-element.13, bf16[2,128]{1,0:T(2,128)(2,1)S(1)} %get-tuple-element.12), kind=kOutput, calls=%fused_computation.15 | convolution fusion | flops 18876416 | bytes 9585664 | tf_op jit(solution)/shard_map/dot_general | solution.py:501
  11.8 0.8 reshape.165.mod_ref
  12.7 166.3 %block.1 = (bf16[2,64,3072]{2,1,0:T(8,128)(2,1)}, f32[8,128]{1,0:T(8,128)}, bf16[2048,3072]{1,0:T(8,128)(2,1)}) custom-call(bf16[2,64,3072]{2,1,0:T(8,128)(2,1)} %bitcast.8, f32[2,6,3072]{2,1,0:T(8,128)} %reshape.165.mod_ref, bf16[2,128,128]{2,1,0:T(8,128)(2,1)} %get-tuple-element.15.tiles_ref, bf16[2,128,128]{2,1,0:T(8,128)(2,1)} %get-tuple-element.14.framesok_ref, ...), custom_call_target="tpu_custom_call" | custom-call | flops 20000000000 | bytes 300000000 | tf_op jit(solution)/shard_map/block/pallas_call | solution.py:453
  179.0 1.2 slice.15
  180.8 2.1 %copy.15 = bf16[2,1,64,3072]{3,2,1,0:T(8,128)(2,1)} copy(bf16[2,1,64,3072]{3,2,1,0:T(8,128)(2,1)} %bitcast.7) | data formatting | bytes 1572864
  (4 shorter events, 0.0 us)
